TPU v7x, 32 devices: a whole 2x2x4 slice. The times are simulated.
32 devices in a mesh: ctx: 16 (over z, y, x), tp: 2 (over core).
Axes of the slice: x: 2, y: 2, z: 4, core: 2. Of those that a mesh axis runs over, the one named last changes fastest.
Arguments:
- tokens: bfloat16 [4, 2048, 1280], P(None, 'ctx'), may hold values from -6 to 6
- cotangent: bfloat16 [4, 2048, 1280], P(None, 'ctx'), may hold values from -6 to 6
- doc_lengths: int32 [4, 8], replicated, may hold values from 1 to 1536, 2048 in all within a row
- w_query: bfloat16 [1280, 1280], P('ctx', 'tp'), may hold values from -0.15625 to 0.15625
- w_key: bfloat16 [1280, 1280], P('ctx', 'tp'), may hold values from -0.15625 to 0.15625
- w_value: bfloat16 [1280, 1280], P('ctx', 'tp'), may hold values from -0.15625 to 0.15625
- w_out: bfloat16 [1280, 1280], P('tp', 'ctx'), may hold values from -0.625 to 0.625
- w_up: bfloat16 [1280, 1280], P('ctx', 'tp'), may hold values from -0.15625 to 0.15625
- w_down: bfloat16 [1280, 1280], P('tp', 'ctx'), may hold values from -0.25 to 0.25
- gain_attn: bfloat16 [1280], P('ctx'), may hold values from 0.099609375 to 1.8984375
- gain_mlp: bfloat16 [1280], P('ctx'), may hold values from 0.099609375 to 1.8984375
- query_scale: float32 [80], replicated, may hold values from 0.06 to 0.3
Outputs:
- layer_out: bfloat16 [4, 2048, 1280], P(None, 'ctx')
- grad_tokens: float32 [4, 2048, 1280], P(None, 'ctx')
- grad_query: float32 [1280, 1280], P('ctx', 'tp')
- grad_key: float32 [1280, 1280], P('ctx', 'tp')
- grad_value: float32 [1280, 1280], P('ctx', 'tp')
- grad_out: float32 [1280, 1280], P('tp', 'ctx')
- grad_up: float32 [1280, 1280], P('ctx', 'tp')
- grad_down: float32 [1280, 1280], P('tp', 'ctx')
- grad_gain_attn: float32 [1280], P('ctx')
- grad_gain_mlp: float32 [1280], P('ctx')
- grad_scale: float32 [80], replicated
Inputs may be any that keep to these rules, and one draw needn't show every extreme that they name: `doc_lengths`: each row holds the lengths of the 8 documents of one stream in order; they sum to 2048, and the longest is exactly 1536.
All inputs are finite; a program needn't handle non-finite values.
Results may differ from a plain program's by a relative error of at most 0.024.
Values may be sent and summed in bfloat16 or wider, within the bound.
No kernel may reach another device: no remote copies, remote signals or barrier semaphores. Data moves between devices by JAX's collectives and lax.ppermute only.
A program may use at most 192 MiB of HBM per device.

v0:
```python
import jax
import jax.numpy as jnp
from jax import lax
from jax.sharding import PartitionSpec as P

EPSILON = 1e-06
MASKED = -1e30


def inverse_rms(values):
    return lax.rsqrt(jnp.mean(values * values, axis=-1, keepdims=True) + EPSILON)


def segment_of(starts, positions):
    return jnp.sum((starts[None, :] <= positions[:, None]).astype(jnp.int32), axis=1)


def contract_rows(left, right):
    return lax.dot_general(
        left, right, (((0,), (0,)), ((), ())), preferred_element_type=jnp.float32
    )


def contract_cols(left, right):
    return lax.dot_general(
        left, right, (((1,), (1,)), ((), ())), preferred_element_type=jnp.float32
    )


def per_device(
    tokens,
    cotangent,
    doc_lengths,
    w_query,
    w_key,
    w_value,
    w_out,
    w_up,
    w_down,
    gain_attn,
    gain_mlp,
    query_scale,
):
    micro_count, tok_rows, model_width = tokens.shape
    head_size = query_scale.shape[0]
    local_cols = w_query.shape[1]
    head_count = local_cols // head_size
    stream = tok_rows * lax.axis_size("ctx")
    key_block = min(512, stream)
    block_count = stream // key_block
    positions = lax.axis_index("ctx") * tok_rows + jnp.arange(tok_rows, dtype=jnp.int32)
    local_sums = None
    scale_sum = jnp.zeros((head_size,), jnp.float32)
    outputs = []
    input_grads = []
    for micro_step in range(micro_count):
        gathered = (
            lax.all_gather(w_query, "ctx", axis=0, tiled=True),
            lax.all_gather(w_key, "ctx", axis=0, tiled=True),
            lax.all_gather(w_value, "ctx", axis=0, tiled=True),
            lax.all_gather(w_up, "ctx", axis=0, tiled=True),
            lax.all_gather(gain_attn, "ctx", axis=0, tiled=True),
            lax.all_gather(gain_mlp, "ctx", axis=0, tiled=True),
            lax.all_gather(w_out, "ctx", axis=1, tiled=True),
            lax.all_gather(w_down, "ctx", axis=1, tiled=True),
        )
        w_qkv = jnp.concatenate([gathered[0], gathered[1], gathered[2]], axis=1)
        up_full = gathered[3]
        gain_one = gathered[4].astype(jnp.float32)
        gain_two = gathered[5].astype(jnp.float32)
        out_full = gathered[6]
        down_full = gathered[7]
        lengths = doc_lengths[micro_step]
        starts = jnp.cumsum(lengths) - lengths
        query_seg = segment_of(starts, positions)
        stream_in = tokens[micro_step].astype(jnp.float32)
        scale_one = inverse_rms(stream_in)
        normed_one = (stream_in * scale_one * gain_one).astype(jnp.bfloat16)
        projected = jnp.dot(normed_one, w_qkv, preferred_element_type=jnp.float32)
        query_raw = projected[:, :local_cols].reshape(tok_rows, head_count, head_size)
        query_heads = (query_raw * query_scale).astype(jnp.bfloat16)
        key_local = projected[:, local_cols : 2 * local_cols].astype(jnp.bfloat16)
        value_local = projected[:, 2 * local_cols :].astype(jnp.bfloat16)
        row_top = jnp.full((head_count, tok_rows), MASKED, jnp.float32)
        key_piece = lax.all_gather(key_local, "ctx", axis=0, tiled=True)
        value_piece = lax.all_gather(value_local, "ctx", axis=0, tiled=True)
        length = key_piece.shape[0]
        key_pos = jnp.arange(length, dtype=jnp.int32)
        allowed = (key_pos[None, :] <= positions[:, None]) & (
            segment_of(starts, key_pos)[None, :] == query_seg[:, None]
        )
        scores = jnp.einsum(
            "qhd,khd->hqk",
            query_heads,
            key_piece.reshape(length, head_count, head_size),
            preferred_element_type=jnp.float32,
        )
        scores = jnp.where(allowed[None], scores, MASKED)
        new_top = jnp.maximum(row_top, jnp.max(scores, axis=-1))
        probs = jnp.where(allowed[None], jnp.exp(scores - new_top[:, :, None]), 0.0)
        row_sum = jnp.sum(probs, axis=-1)
        update = jnp.einsum(
            "hqk,khd->qhd",
            probs.astype(jnp.bfloat16),
            value_piece.reshape(length, head_count, head_size),
            preferred_element_type=jnp.float32,
        )
        weighted = update
        row_top, row_sum, weighted = (new_top, row_sum, weighted)
        attn_heads = weighted / jnp.transpose(row_sum)[:, :, None]
        log_total = row_top + jnp.log(row_sum)
        attn_low = attn_heads.reshape(tok_rows, local_cols).astype(jnp.bfloat16)
        attn_out = lax.psum(
            jnp.dot(attn_low, out_full, preferred_element_type=jnp.float32).astype(jnp.bfloat16),
            "tp",
        ).astype(jnp.float32)
        hidden = stream_in + attn_out
        scale_two = inverse_rms(hidden)
        normed_two = (hidden * scale_two * gain_two).astype(jnp.bfloat16)
        up_raw = jnp.dot(normed_two, up_full, preferred_element_type=jnp.float32)
        activated = jax.nn.silu(up_raw).astype(jnp.bfloat16)
        mlp_out = lax.psum(
            jnp.dot(activated, down_full, preferred_element_type=jnp.float32).astype(jnp.bfloat16),
            "tp",
        ).astype(jnp.float32)
        outputs.append((hidden + mlp_out).astype(jnp.bfloat16))
        grad_out = cotangent[micro_step]
        grad_down = contract_rows(activated, grad_out)
        grad_act = contract_cols(grad_out, down_full)
        sigma = jax.nn.sigmoid(up_raw)
        grad_up_raw = (grad_act * sigma * (1.0 + up_raw * (1.0 - sigma))).astype(jnp.bfloat16)
        grad_up = contract_rows(normed_two, grad_up_raw)
        grad_normed_two = lax.psum(
            contract_cols(grad_up_raw, up_full).astype(jnp.bfloat16), "tp"
        ).astype(jnp.float32)
        grad_gain_two = jnp.sum(grad_normed_two * hidden * scale_two, axis=0)
        weighted_two = grad_normed_two * gain_two
        grad_hidden = (
            grad_out.astype(jnp.float32)
            + scale_two * weighted_two
            - hidden * scale_two**3 * jnp.mean(weighted_two * hidden, axis=-1, keepdims=True)
        )
        hidden_low = grad_hidden.astype(jnp.bfloat16)
        grad_out_proj = contract_rows(attn_low, hidden_low)
        grad_attn = (
            contract_cols(hidden_low, out_full)
            .astype(jnp.bfloat16)
            .reshape(tok_rows, head_count, head_size)
        )
        delta = jnp.einsum("qhd,qhd->hq", grad_attn.astype(jnp.float32), attn_heads)
        key_all, value_all = (
            lax.all_gather(key_local, "ctx", axis=0, tiled=True),
            lax.all_gather(value_local, "ctx", axis=0, tiled=True),
        )

        def block_terms(key_piece, value_piece, offset):
            key_heads = key_piece.reshape(key_block, head_count, head_size)
            value_heads = value_piece.reshape(key_block, head_count, head_size)
            key_pos = offset + jnp.arange(key_block, dtype=jnp.int32)
            allowed = (key_pos[None, :] <= positions[:, None]) & (
                segment_of(starts, key_pos)[None, :] == query_seg[:, None]
            )
            scores = jnp.einsum(
                "qhd,khd->hqk", query_heads, key_heads, preferred_element_type=jnp.float32
            )
            probs = jnp.where(allowed[None], jnp.exp(scores - log_total[:, :, None]), 0.0)
            grad_probs = jnp.einsum(
                "qhd,khd->hqk", grad_attn, value_heads, preferred_element_type=jnp.float32
            )
            grad_scores = (probs * (grad_probs - delta[:, :, None])).astype(jnp.bfloat16)
            return (key_heads, probs, grad_scores)

        key_blocks = (
            key_all.reshape(block_count, key_block, local_cols),
            value_all.reshape(block_count, key_block, local_cols),
            jnp.arange(block_count, dtype=jnp.int32) * key_block,
        )
        zero_query = jnp.zeros((tok_rows, head_count, head_size), jnp.float32)

        def grad_block(grad_query, packed):
            key_heads, probs, grad_scores = block_terms(packed[0], packed[1], packed[2])
            grad_value = jnp.einsum(
                "hqk,qhd->khd",
                probs.astype(jnp.bfloat16),
                grad_attn,
                preferred_element_type=jnp.float32,
            )
            grad_query = grad_query + jnp.einsum(
                "hqk,khd->qhd", grad_scores, key_heads, preferred_element_type=jnp.float32
            )
            grad_key = jnp.einsum(
                "hqk,qhd->khd", grad_scores, query_heads, preferred_element_type=jnp.float32
            )
            return (
                grad_query,
                (
                    grad_key.reshape(key_block, local_cols),
                    grad_value.reshape(key_block, local_cols),
                ),
            )

        grad_query, (key_terms, value_terms) = lax.scan(grad_block, zero_query, key_blocks)
        key_grad, value_grad = (
            lax.psum_scatter(
                key_terms.reshape(stream, local_cols).astype(jnp.bfloat16),
                "ctx",
                scatter_dimension=0,
                tiled=True,
            ).astype(jnp.float32),
            lax.psum_scatter(
                value_terms.reshape(stream, local_cols).astype(jnp.bfloat16),
                "ctx",
                scatter_dimension=0,
                tiled=True,
            ).astype(jnp.float32),
        )
        grad_query_raw = (
            (grad_query * query_scale).astype(jnp.bfloat16).reshape(tok_rows, local_cols)
        )
        scale_part = jnp.sum(grad_query * query_raw, axis=(0, 1))
        grad_cols = jnp.concatenate(
            [grad_query_raw, key_grad.astype(jnp.bfloat16), value_grad.astype(jnp.bfloat16)], axis=1
        )
        grad_qkv = contract_rows(normed_one, grad_cols)
        grad_normed_one, scale_total = (
            lax.psum(contract_cols(grad_cols, w_qkv).astype(jnp.bfloat16), "tp").astype(
                jnp.float32
            ),
            lax.psum(scale_part.astype(jnp.bfloat16), "tp").astype(jnp.float32),
        )
        scale_sum = scale_sum + scale_total
        grad_gain_one = jnp.sum(grad_normed_one * stream_in * scale_one, axis=0)
        weighted_one = grad_normed_one * gain_one
        input_grads.append(
            grad_hidden
            + scale_one * weighted_one
            - stream_in * scale_one**3 * jnp.mean(weighted_one * stream_in, axis=-1, keepdims=True)
        )
        grads = (
            grad_qkv[:, :local_cols],
            grad_qkv[:, local_cols : 2 * local_cols],
            grad_qkv[:, 2 * local_cols :],
            grad_up,
            grad_gain_one,
            grad_gain_two,
            grad_out_proj,
            grad_down,
        )
        shares = (
            lax.psum_scatter(
                grads[0].astype(jnp.bfloat16), "ctx", scatter_dimension=0, tiled=True
            ).astype(jnp.float32),
            lax.psum_scatter(
                grads[1].astype(jnp.bfloat16), "ctx", scatter_dimension=0, tiled=True
            ).astype(jnp.float32),
            lax.psum_scatter(
                grads[2].astype(jnp.bfloat16), "ctx", scatter_dimension=0, tiled=True
            ).astype(jnp.float32),
            lax.psum_scatter(
                grads[3].astype(jnp.bfloat16), "ctx", scatter_dimension=0, tiled=True
            ).astype(jnp.float32),
            lax.psum_scatter(
                grads[4].astype(jnp.bfloat16), "ctx", scatter_dimension=0, tiled=True
            ).astype(jnp.float32),
            lax.psum_scatter(
                grads[5].astype(jnp.bfloat16), "ctx", scatter_dimension=0, tiled=True
            ).astype(jnp.float32),
            lax.psum_scatter(
                grads[6].astype(jnp.bfloat16), "ctx", scatter_dimension=1, tiled=True
            ).astype(jnp.float32),
            lax.psum_scatter(
                grads[7].astype(jnp.bfloat16), "ctx", scatter_dimension=1, tiled=True
            ).astype(jnp.float32),
        )
        local_sums = (
            shares
            if local_sums is None
            else tuple((total + extra for total, extra in zip(local_sums, shares)))
        )
    scale_grad = lax.psum(scale_sum, "ctx")
    return (
        jnp.stack(outputs),
        jnp.stack(input_grads),
        local_sums[0],
        local_sums[1],
        local_sums[2],
        local_sums[6],
        local_sums[3],
        local_sums[7],
        local_sums[4],
        local_sums[5],
        scale_grad,
    )


def solution(mesh):
    in_specs = (
        P(None, "ctx", None),
        P(None, "ctx", None),
        P(),
        P("ctx", "tp"),
        P("ctx", "tp"),
        P("ctx", "tp"),
        P("tp", "ctx"),
        P("ctx", "tp"),
        P("tp", "ctx"),
        P("ctx"),
        P("ctx"),
        P(),
    )
    out_specs = (
        P(None, "ctx", None),
        P(None, "ctx", None),
        P("ctx", "tp"),
        P("ctx", "tp"),
        P("ctx", "tp"),
        P("tp", "ctx"),
        P("ctx", "tp"),
        P("tp", "ctx"),
        P("ctx"),
        P("ctx"),
        P(),
    )
    return jax.shard_map(
        per_device, mesh=mesh, in_specs=in_specs, out_specs=out_specs, check_vma=False
    )
```

profile of v0, /device:TPU:0, one launch (start us, length us, event | category | flops | bytes accessed | tf_op | source)
XLA Modules:
  0.0 3650.7 jit_solution(5075666711736154191)
XLA Ops:
  1411.1 76.5 %reduce-scatter.39.cloned.1.call-done = bf16[128,640]{1,0:T(8,128)(2,1)} async-done(((bf16[2048,640]{1,0:T(8,128)(2,1)}), bf16[128,640]{1,0:T(8,128)(2,1)}) %reduce-scatter.39.cloned.1.call-update) | async-done | bytes 163856 | tf_op jit(solution)/shard_map/reduce_scatter | solution.py:210
  1487.6 82.2 %reduce-scatter.37.cloned.1.call-done = bf16[128,640]{1,0:T(8,128)(2,1)} async-done(((bf16[2048,640]{1,0:T(8,128)(2,1)}), bf16[128,640]{1,0:T(8,128)(2,1)}) %reduce-scatter.37.cloned.1.call-update) | async-done | bytes 163856 | tf_op jit(solution)/shard_map/reduce_scatter | solution.py:204
  1574.6 76.9 %reduce-scatter.43.cloned.1.call-done = bf16[128,640]{1,0:T(8,128)(2,1)} async-done(((bf16[2048,640]{1,0:T(8,128)(2,1)}), bf16[128,640]{1,0:T(8,128)(2,1)}) %reduce-scatter.43.cloned.1.call-update) | async-done | bytes 163856 | tf_op jit(solution)/shard_map/reduce_scatter | solution.py:210
  1651.5 81.9 %reduce-scatter.41.cloned.1.call-done = bf16[128,640]{1,0:T(8,128)(2,1)} async-done(((bf16[2048,640]{1,0:T(8,128)(2,1)}), bf16[128,640]{1,0:T(8,128)(2,1)}) %reduce-scatter.41.cloned.1.call-update) | async-done | bytes 163856 | tf_op jit(solution)/shard_map/reduce_scatter | solution.py:204
  1812.3 78.3 %reduce-scatter.87.cloned.1.call-done = bf16[80,640]{1,0:T(8,128)(2,1)} async-done(((bf16[1280,640]{1,0:T(8,128)(2,1)}), bf16[80,640]{1,0:T(8,128)(2,1)}) %reduce-scatter.87.cloned.1.call-update) | async-done | bytes 102416 | tf_op jit(solution)/shard_map/reduce_scatter | solution.py:259
  1890.6 78.3 %reduce-scatter.83.cloned.1.call-done = bf16[80,640]{1,0:T(8,128)(2,1)} async-done(((bf16[1280,640]{1,0:T(8,128)(2,1)}), bf16[80,640]{1,0:T(8,128)(2,1)}) %reduce-scatter.83.cloned.1.call-update) | async-done | bytes 102416 | tf_op jit(solution)/shard_map/reduce_scatter | solution.py:259
  1968.9 78.5 %reduce-scatter.81.cloned.1.call-done = bf16[80,640]{1,0:T(8,128)(2,1)} async-done(((bf16[1280,640]{1,0:T(8,128)(2,1)}), bf16[80,640]{1,0:T(8,128)(2,1)}) %reduce-scatter.81.cloned.1.call-update) | async-done | bytes 102416 | tf_op jit(solution)/shard_map/reduce_scatter | solution.py:259
  2049.1 76.8 %reduce-scatter.93.cloned.1.call-done = bf16[640,80]{0,1:T(8,128)(2,1)} async-done(((bf16[640,1280]{0,1:T(8,128)(2,1)}), bf16[640,80]{0,1:T(8,128)(2,1)}) %reduce-scatter.93.cloned.1.call-update) | async-done | bytes 102416 | tf_op jit(solution)/shard_map/reduce_scatter | solution.py:271
  2125.9 78.3 %reduce-scatter.95.cloned.1.call-done = bf16[640,80]{0,1:T(8,128)(2,1)} async-done(((bf16[640,1280]{0,1:T(8,128)(2,1)}), bf16[640,80]{0,1:T(8,128)(2,1)}) %reduce-scatter.95.cloned.1.call-update) | async-done | bytes 102416 | tf_op jit(solution)/shard_map/reduce_scatter | solution.py:271
  2204.2 78.5 %reduce-scatter.91.cloned.1.call-done = bf16[640,80]{0,1:T(8,128)(2,1)} async-done(((bf16[640,1280]{0,1:T(8,128)(2,1)}), bf16[640,80]{0,1:T(8,128)(2,1)}) %reduce-scatter.91.cloned.1.call-update) | async-done | bytes 102416 | tf_op jit(solution)/shard_map/reduce_scatter | solution.py:271
  2282.7 78.2 %reduce-scatter.89.cloned.1.call-done = bf16[640,80]{0,1:T(8,128)(2,1)} async-done(((bf16[640,1280]{0,1:T(8,128)(2,1)}), bf16[640,80]{0,1:T(8,128)(2,1)}) %reduce-scatter.89.cloned.1.call-update) | async-done | bytes 102416 | tf_op jit(solution)/shard_map/reduce_scatter | solution.py:271
  2439.1 78.5 %reduce-scatter.77.cloned.1.call-done = bf16[640,80]{0,1:T(8,128)(2,1)} async-done(((bf16[640,1280]{0,1:T(8,128)(2,1)}), bf16[640,80]{0,1:T(8,128)(2,1)}) %reduce-scatter.77.cloned.1.call-update) | async-done | bytes 102416 | tf_op jit(solution)/shard_map/reduce_scatter | solution.py:268
  2517.6 78.4 %reduce-scatter.75.cloned.1.call-done = bf16[640,80]{0,1:T(8,128)(2,1)} async-done(((bf16[640,1280]{0,1:T(8,128)(2,1)}), bf16[640,80]{0,1:T(8,128)(2,1)}) %reduce-scatter.75.cloned.1.call-update) | async-done | bytes 102416 | tf_op jit(solution)/shard_map/reduce_scatter | solution.py:268
  2596.0 78.4 %reduce-scatter.73.cloned.1.call-done = bf16[640,80]{0,1:T(8,128)(2,1)} async-done(((bf16[640,1280]{0,1:T(8,128)(2,1)}), bf16[640,80]{0,1:T(8,128)(2,1)}) %reduce-scatter.73.cloned.1.call-update) | async-done | bytes 102416 | tf_op jit(solution)/shard_map/reduce_scatter | solution.py:268
  2699.2 77.6 %all-reduce.10 = (bf16[1280]{0:T(1024)(128)(2,1)S(1)}, bf16[1280]{0:T(1024)(128)(2,1)S(1)}, bf16[1280]{0:T(1024)(128)(2,1)S(1)}, bf16[1280]{0:T(1024)(128)(2,1)S...) all-reduce(bf16[1280]{0:T(1024)(128)(2,1)S(1)} %get-tuple-element.7, ...), channel_id=37, replica_groups=mesh['ctx'=16,'tp'=2] {'ctx'}, use_global_device_ids=true, to_apply=%region_103.104.clone | all-reduce | flops 10240 | bytes 40960
  2858.6 78.2 %reduce-scatter.51.cloned.1.call-done = bf16[80,640]{1,0:T(8,128)(2,1)} async-done(((bf16[1280,640]{1,0:T(8,128)(2,1)}), bf16[80,640]{1,0:T(8,128)(2,1)}) %reduce-scatter.51.cloned.1.call-update) | async-done | bytes 102416 | tf_op jit(solution)/shard_map/reduce_scatter | solution.py:250
  2936.8 78.5 %reduce-scatter.49.cloned.1.call-done = bf16[80,640]{1,0:T(8,128)(2,1)} async-done(((bf16[1280,640]{1,0:T(8,128)(2,1)}), bf16[80,640]{1,0:T(8,128)(2,1)}) %reduce-scatter.49.cloned.1.call-update) | async-done | bytes 102416 | tf_op jit(solution)/shard_map/reduce_scatter | solution.py:250
  3017.1 76.8 %reduce-scatter.63.cloned.1.call-done = bf16[80,640]{1,0:T(8,128)(2,1)} async-done(((bf16[1280,640]{1,0:T(8,128)(2,1)}), bf16[80,640]{1,0:T(8,128)(2,1)}) %reduce-scatter.63.cloned.1.call-update) | async-done | bytes 102416 | tf_op jit(solution)/shard_map/reduce_scatter | solution.py:253
  3093.8 78.4 %reduce-scatter.61.cloned.1.call-done = bf16[80,640]{1,0:T(8,128)(2,1)} async-done(((bf16[1280,640]{1,0:T(8,128)(2,1)}), bf16[80,640]{1,0:T(8,128)(2,1)}) %reduce-scatter.61.cloned.1.call-update) | async-done | bytes 102416 | tf_op jit(solution)/shard_map/reduce_scatter | solution.py:253
  3172.2 78.3 %reduce-scatter.59.cloned.1.call-done = bf16[80,640]{1,0:T(8,128)(2,1)} async-done(((bf16[1280,640]{1,0:T(8,128)(2,1)}), bf16[80,640]{1,0:T(8,128)(2,1)}) %reduce-scatter.59.cloned.1.call-update) | async-done | bytes 102416 | tf_op jit(solution)/shard_map/reduce_scatter | solution.py:253
  3250.6 78.3 %reduce-scatter.57.cloned.1.call-done = bf16[80,640]{1,0:T(8,128)(2,1)} async-done(((bf16[1280,640]{1,0:T(8,128)(2,1)}), bf16[80,640]{1,0:T(8,128)(2,1)}) %reduce-scatter.57.cloned.1.call-update) | async-done | bytes 102416 | tf_op jit(solution)/shard_map/reduce_scatter | solution.py:253
  3406.9 78.6 %reduce-scatter.69.cloned.1.call-done = bf16[80,640]{1,0:T(8,128)(2,1)} async-done(((bf16[1280,640]{1,0:T(8,128)(2,1)}), bf16[80,640]{1,0:T(8,128)(2,1)}) %reduce-scatter.69.cloned.1.call-update) | async-done | bytes 102416 | tf_op jit(solution)/shard_map/reduce_scatter | solution.py:256
  3485.5 78.2 %reduce-scatter.67.cloned.1.call-done = bf16[80,640]{1,0:T(8,128)(2,1)} async-done(((bf16[1280,640]{1,0:T(8,128)(2,1)}), bf16[80,640]{1,0:T(8,128)(2,1)}) %reduce-scatter.67.cloned.1.call-update) | async-done | bytes 102416 | tf_op jit(solution)/shard_map/reduce_scatter | solution.py:256
  3563.7 78.5 %reduce-scatter.65.cloned.1.call-done = bf16[80,640]{1,0:T(8,128)(2,1)} async-done(((bf16[1280,640]{1,0:T(8,128)(2,1)}), bf16[80,640]{1,0:T(8,128)(2,1)}) %reduce-scatter.65.cloned.1.call-update) | async-done | bytes 102416 | tf_op jit(solution)/shard_map/reduce_scatter | solution.py:256
  (1033 shorter events, 2034.7 us)
Async XLA Ops:
  1319.4 571.2 %reduce-scatter.87.cloned.1.call-start = ((), (), s32[]{:S(2)}) async-start(), calls=%async_computation.74 | async-start | bytes 1740800 | tf_op jit(solution)/shard_map/reduce_scatter | solution.py:259
  1321.4 647.5 %reduce-scatter.83.cloned.1.call-start = ((), (), s32[]{:S(2)}) async-start(), calls=%async_computation.72 | async-start | bytes 1740800 | tf_op jit(solution)/shard_map/reduce_scatter | solution.py:259
  1323.4 724.0 %reduce-scatter.81.cloned.1.call-start = ((), (), s32[]{:S(2)}) async-start(), calls=%async_computation.71 | async-start | bytes 1740800 | tf_op jit(solution)/shard_map/reduce_scatter | solution.py:259
  1325.8 800.1 %reduce-scatter.93.cloned.1.call-start = ((), (), s32[]{:S(2)}) async-start(), calls=%async_computation.77 | async-start | bytes 1740800 | tf_op jit(solution)/shard_map/reduce_scatter | solution.py:271
  1328.7 875.5 %reduce-scatter.95.cloned.1.call-start = ((), (), s32[]{:S(2)}) async-start(), calls=%async_computation.78 | async-start | bytes 1740800 | tf_op jit(solution)/shard_map/reduce_scatter | solution.py:271
  1331.6 951.1 %reduce-scatter.91.cloned.1.call-start = ((), (), s32[]{:S(2)}) async-start(), calls=%async_computation.76 | async-start | bytes 1740800 | tf_op jit(solution)/shard_map/reduce_scatter | solution.py:271
  1334.5 1026.4 %reduce-scatter.89.cloned.1.call-start = ((), (), s32[]{:S(2)}) async-start(), calls=%async_computation.75 | async-start | bytes 1740800 | tf_op jit(solution)/shard_map/reduce_scatter | solution.py:271
  1337.5 1101.6 %reduce-scatter.79.cloned.1.call-start = ((), (), s32[]{:S(2)}) async-start(), calls=%async_computation.70 | async-start | bytes 1740800 | tf_op jit(solution)/shard_map/reduce_scatter | solution.py:268
  1340.5 1177.1 %reduce-scatter.77.cloned.1.call-start = ((), (), s32[]{:S(2)}) async-start(), calls=%async_computation.69 | async-start | bytes 1740800 | tf_op jit(solution)/shard_map/reduce_scatter | solution.py:268
  1343.5 1252.5 %reduce-scatter.75.cloned.1.call-start = ((), (), s32[]{:S(2)}) async-start(), calls=%async_computation.68 | async-start | bytes 1740800 | tf_op jit(solution)/shard_map/reduce_scatter | solution.py:268
  1346.3 1328.1 %reduce-scatter.73.cloned.1.call-start = ((), (), s32[]{:S(2)}) async-start(), calls=%async_computation.67 | async-start | bytes 1740800 | tf_op jit(solution)/shard_map/reduce_scatter | solution.py:268
  1351.0 1346.1 %all-reduce.23.cloned.1.call-start = ((), (), s32[]{:S(2)}) async-start(), calls=%async_computation.79 | async-start | bytes 5242880 | tf_op jit(solution)/shard_map/psum | solution.py:122
  1738.3 1046.4 %reduce-scatter.55.cloned.1.call-start = ((), (), s32[]{:S(2)}) async-start(), calls=%async_computation.58 | async-start | bytes 1740800 | tf_op jit(solution)/shard_map/reduce_scatter | solution.py:250
  1743.2 1115.3 %reduce-scatter.53.cloned.1.call-start = ((), (), s32[]{:S(2)}) async-start(), calls=%async_computation.57 | async-start | bytes 1740800 | tf_op jit(solution)/shard_map/reduce_scatter | solution.py:250
  1747.4 1189.4 %reduce-scatter.51.cloned.1.call-start = ((), (), s32[]{:S(2)}) async-start(), calls=%async_computation.56 | async-start | bytes 1740800 | tf_op jit(solution)/shard_map/reduce_scatter | solution.py:250
  1751.4 1263.9 %reduce-scatter.49.cloned.1.call-start = ((), (), s32[]{:S(2)}) async-start(), calls=%async_computation.55 | async-start | bytes 1740800 | tf_op jit(solution)/shard_map/reduce_scatter | solution.py:250
  1755.4 1338.4 %reduce-scatter.63.cloned.1.call-start = ((), (), s32[]{:S(2)}) async-start(), calls=%async_computation.62 | async-start | bytes 1740800 | tf_op jit(solution)/shard_map/reduce_scatter | solution.py:253
  1756.0 1416.2 %reduce-scatter.61.cloned.1.call-start = ((), (), s32[]{:S(2)}) async-start(), calls=%async_computation.61 | async-start | bytes 1740800 | tf_op jit(solution)/shard_map/reduce_scatter | solution.py:253
  1756.8 1493.8 %reduce-scatter.59.cloned.1.call-start = ((), (), s32[]{:S(2)}) async-start(), calls=%async_computation.60 | async-start | bytes 1740800 | tf_op jit(solution)/shard_map/reduce_scatter | solution.py:253
  1757.3 1571.6 %reduce-scatter.57.cloned.1.call-start = ((), (), s32[]{:S(2)}) async-start(), calls=%async_computation.59 | async-start | bytes 1740800 | tf_op jit(solution)/shard_map/reduce_scatter | solution.py:253
  1757.9 1649.0 %reduce-scatter.71.cloned.1.call-start = ((), (), s32[]{:S(2)}) async-start(), calls=%async_computation.66 | async-start | bytes 1740800 | tf_op jit(solution)/shard_map/reduce_scatter | solution.py:256
  1758.5 1727.0 %reduce-scatter.69.cloned.1.call-start = ((), (), s32[]{:S(2)}) async-start(), calls=%async_computation.65 | async-start | bytes 1740800 | tf_op jit(solution)/shard_map/reduce_scatter | solution.py:256
  1759.1 1804.6 %reduce-scatter.67.cloned.1.call-start = ((), (), s32[]{:S(2)}) async-start(), calls=%async_computation.64 | async-start | bytes 1740800 | tf_op jit(solution)/shard_map/reduce_scatter | solution.py:256
  1759.7 1882.5 %reduce-scatter.65.cloned.1.call-start = ((), (), s32[]{:S(2)}) async-start(), calls=%async_computation.63 | async-start | bytes 1740800 | tf_op jit(solution)/shard_map/reduce_scatter | solution.py:256
  (248 other events, 10823.8 us)
Sparse Core Ops, SparseCore 0:
  1076.9 83.4 reduce-scatter.46
  1163.4 79.0 reduce-scatter.44
  1244.8 79.4 reduce-scatter.34
  1326.7 79.6 reduce-scatter.32
  1408.7 78.8 reduce-scatter.38
  1490.0 79.7 reduce-scatter.36
  1572.1 79.4 reduce-scatter.42
  1653.9 79.4 reduce-scatter.40
  1735.7 76.5 reduce-scatter.84
  1814.4 76.1 reduce-scatter.86
  1971.2 76.1 reduce-scatter.80
  2049.6 76.2 reduce-scatter.92
  2206.6 76.0 reduce-scatter.90
  2284.8 76.0 reduce-scatter.88
  2441.4 76.1 reduce-scatter.76
  2519.8 76.0 reduce-scatter.74
  2598.1 76.2 reduce-scatter.72
  2699.2 80.8 reduce-scatter.54
  2939.2 76.0 reduce-scatter.48
  3017.4 76.3 reduce-scatter.62
  3174.4 76.1 reduce-scatter.58
  3252.8 76.0 reduce-scatter.56
  3409.1 76.3 reduce-scatter.68
  3566.1 76.0 reduce-scatter.64
  (26 shorter events, 1533.6 us)
where the time goes:
time: 3670 us; the launch traced here: 3650 us
  waiting for transfers between devices  2880 us (78%)
  matrix products  254 us (7%)
  local copies, waits for them, and re-layouts  219 us (6%)
  blocking collectives  163 us (4%)
  other arithmetic  99 us (3%)
    reduce_scatter x4, waiting for transfers between devices, per_device(): lax.psum_scatter(grads[1].astype(jnp.bfloat16), 'ctx', scatter_dimension=...  312 us
    reduce_scatter x4, waiting for transfers between devices, per_device(): lax.psum_scatter(grads[7].astype(jnp.bfloat16), 'ctx', scatter_dimension=...  312 us
    reduce_scatter x4, waiting for transfers between devices, per_device(): lax.psum_scatter(grads[6].astype(jnp.bfloat16), 'ctx', scatter_dimension=...  312 us
    reduce_scatter x4, waiting for transfers between devices, per_device(): lax.psum_scatter(grads[2].astype(jnp.bfloat16), 'ctx', scatter_dimension=...  311 us
    reduce_scatter x4, waiting for transfers between devices, per_device(): lax.psum_scatter(grads[3].astype(jnp.bfloat16), 'ctx', scatter_dimension=...  246 us
    all_gather x4, waiting for transfers between devices, per_device(): key_piece = lax.all_gather(key_local, 'ctx', axis=0, tiled=True)  239 us
    reduce_scatter x4, waiting for transfers between devices, per_device(): lax.psum_scatter(grads[0].astype(jnp.bfloat16), 'ctx', scatter_dimension=...  231 us
    all_gather x4, waiting for transfers between devices, per_device(): value_piece = lax.all_gather(value_local, 'ctx', axis=0, tiled=True)  217 us
  transfers between devices with their start and end apart: 50, of which 46 were waited for; matrix products, arithmetic and copies ran while one was open for 12% of the time, Pallas kernels for 0%

commit v1 on v0

--- a/solution.py
+++ b/solution.py
@@ -82,8 +82,13 @@
         key_local = projected[:, local_cols : 2 * local_cols].astype(jnp.bfloat16)
         value_local = projected[:, 2 * local_cols :].astype(jnp.bfloat16)
         row_top = jnp.full((head_count, tok_rows), MASKED, jnp.float32)
-        key_piece = lax.all_gather(key_local, "ctx", axis=0, tiled=True)
-        value_piece = lax.all_gather(value_local, "ctx", axis=0, tiled=True)
+        key_piece, value_piece = jnp.split(
+            lax.all_gather(
+                jnp.concatenate([key_local, value_local], 1), axis_name="ctx", axis=0, tiled=True
+            ),
+            [key_local.shape[1]],
+            1,
+        )
         length = key_piece.shape[0]
         key_pos = jnp.arange(length, dtype=jnp.int32)
         allowed = (key_pos[None, :] <= positions[:, None]) & (

time: 3670 us -> 3960 us (1.079)
  waiting for transfers between devices: 2880 us -> 3170 us
    all_gather x8 -> x12, waiting for transfers between devices: 456 us -> 589 us  [the longest x4 297 us: per_device(): lax.all_gather(jnp.concatenate([key_local, value_local], 1), axis_name='c...]
    reduce_scatter x4, waiting for transfers between devices: 204 us -> 290 us  [per_device(): lax.psum_scatter(key_terms.reshape(stream, local_cols).astype(jnp.bfloat1...]
    reduce_scatter x4, waiting for transfers between devices: 153 us -> 231 us  [per_device(): lax.psum_scatter(value_terms.reshape(stream, local_cols).astype(jnp.bfloa...]
    split x0 -> x12, local copies, waits for them, and re-layouts: none -> 57 us  [per_device(): jnp.split(lax.all_gather(jnp.concatenate([key_local, value_local], 1), ax...]
  transfers between devices with their start and end apart: 50 -> 54, of which waited for: 46 -> 49; matrix products, arithmetic and copies ran while one was open for 12% -> 13% of each run, Pallas kernels for 0% -> 0%
where the time goes in v1:
time: 3960 us; the launch traced here: 3950 us
  waiting for transfers between devices  3170 us (80%)
  matrix products  258 us (7%)
  local copies, waits for them, and re-layouts  248 us (6%)
  blocking collectives  162 us (4%)
  other arithmetic  88.9 us (2%)
    reduce_scatter x4, waiting for transfers between devices, per_device(): lax.psum_scatter(grads[6].astype(jnp.bfloat16), 'ctx', scatter_dimension=...  312 us
    reduce_scatter x4, waiting for transfers between devices, per_device(): lax.psum_scatter(grads[7].astype(jnp.bfloat16), 'ctx', scatter_dimension=...  312 us
    reduce_scatter x4, waiting for transfers between devices, per_device(): lax.psum_scatter(grads[1].astype(jnp.bfloat16), 'ctx', scatter_dimension=...  311 us
    reduce_scatter x4, waiting for transfers between devices, per_device(): lax.psum_scatter(grads[2].astype(jnp.bfloat16), 'ctx', scatter_dimension=...  311 us
    all_gather x4, waiting for transfers between devices, per_device(): lax.all_gather(jnp.concatenate([key_local, value_local], 1), axis_name='c...  297 us
    reduce_scatter x4, waiting for transfers between devices, per_device(): lax.psum_scatter(key_terms.reshape(stream, local_cols).astype(jnp.bfloat1...  290 us
    reduce_scatter x4, waiting for transfers between devices, per_device(): lax.psum_scatter(grads[3].astype(jnp.bfloat16), 'ctx', scatter_dimension=...  245 us
    reduce_scatter x4, waiting for transfers between devices, per_device(): lax.psum_scatter(value_terms.reshape(stream, local_cols).astype(jnp.bfloa...  231 us
  transfers between devices with their start and end apart: 54, of which 49 were waited for; matrix products, arithmetic and copies ran while one was open for 13% of the time, Pallas kernels for 0%

profile of v1, /device:TPU:0, one launch (start us, length us, event | category | flops | bytes accessed | tf_op | source)
XLA Modules:
  0.0 3948.8 jit_solution(11535970523160682145)
XLA Ops:
  202.8 80.4 %all-gather.35.cloned.1.call-done = bf16[2048,1280]{1,0:T(8,128)(2,1)} async-done(((bf16[128,1280]{1,0:T(8,128)(2,1)}), bf16[2048,1280]{1,0:T(8,128)(2,1)}) %all-gather.35.cloned.1.call-update) | async-done | bytes 5242896 | tf_op jit(solution)/shard_map/all_gather | solution.py:86
  489.0 83.2 %all-gather.37.cloned.1.call-done = bf16[2048,1280]{1,0:T(8,128)(2,1)} async-done(((bf16[128,1280]{1,0:T(8,128)(2,1)}), bf16[2048,1280]{1,0:T(8,128)(2,1)}) %all-gather.37.cloned.1.call-update) | async-done | bytes 5242896 | tf_op jit(solution)/shard_map/all_gather | solution.py:86
  1622.7 82.1 %reduce-scatter.33.cloned.1.call-done = bf16[128,640]{1,0:T(8,128)(2,1)} async-done(((bf16[2048,640]{1,0:T(8,128)(2,1)}), bf16[128,640]{1,0:T(8,128)(2,1)}) %reduce-scatter.33.cloned.1.call-update) | async-done | bytes 163856 | tf_op jit(solution)/shard_map/reduce_scatter | solution.py:209
  1786.3 81.5 %reduce-scatter.37.cloned.1.call-done = bf16[128,640]{1,0:T(8,128)(2,1)} async-done(((bf16[2048,640]{1,0:T(8,128)(2,1)}), bf16[128,640]{1,0:T(8,128)(2,1)}) %reduce-scatter.37.cloned.1.call-update) | async-done | bytes 163856 | tf_op jit(solution)/shard_map/reduce_scatter | solution.py:209
  1872.7 77.2 %reduce-scatter.43.cloned.1.call-done = bf16[128,640]{1,0:T(8,128)(2,1)} async-done(((bf16[2048,640]{1,0:T(8,128)(2,1)}), bf16[128,640]{1,0:T(8,128)(2,1)}) %reduce-scatter.43.cloned.1.call-update) | async-done | bytes 163856 | tf_op jit(solution)/shard_map/reduce_scatter | solution.py:215
  1949.8 82.0 %reduce-scatter.41.cloned.1.call-done = bf16[128,640]{1,0:T(8,128)(2,1)} async-done(((bf16[2048,640]{1,0:T(8,128)(2,1)}), bf16[128,640]{1,0:T(8,128)(2,1)}) %reduce-scatter.41.cloned.1.call-update) | async-done | bytes 163856 | tf_op jit(solution)/shard_map/reduce_scatter | solution.py:209
  2110.4 78.4 %reduce-scatter.87.cloned.1.call-done = bf16[80,640]{1,0:T(8,128)(2,1)} async-done(((bf16[1280,640]{1,0:T(8,128)(2,1)}), bf16[80,640]{1,0:T(8,128)(2,1)}) %reduce-scatter.87.cloned.1.call-update) | async-done | bytes 102416 | tf_op jit(solution)/shard_map/reduce_scatter | solution.py:264
  2188.9 78.4 %reduce-scatter.83.cloned.1.call-done = bf16[80,640]{1,0:T(8,128)(2,1)} async-done(((bf16[1280,640]{1,0:T(8,128)(2,1)}), bf16[80,640]{1,0:T(8,128)(2,1)}) %reduce-scatter.83.cloned.1.call-update) | async-done | bytes 102416 | tf_op jit(solution)/shard_map/reduce_scatter | solution.py:264
  2267.2 78.3 %reduce-scatter.81.cloned.1.call-done = bf16[80,640]{1,0:T(8,128)(2,1)} async-done(((bf16[1280,640]{1,0:T(8,128)(2,1)}), bf16[80,640]{1,0:T(8,128)(2,1)}) %reduce-scatter.81.cloned.1.call-update) | async-done | bytes 102416 | tf_op jit(solution)/shard_map/reduce_scatter | solution.py:264
  2423.9 78.4 %reduce-scatter.95.cloned.1.call-done = bf16[640,80]{0,1:T(8,128)(2,1)} async-done(((bf16[640,1280]{0,1:T(8,128)(2,1)}), bf16[640,80]{0,1:T(8,128)(2,1)}) %reduce-scatter.95.cloned.1.call-update) | async-done | bytes 102416 | tf_op jit(solution)/shard_map/reduce_scatter | solution.py:276
  2502.3 78.3 %reduce-scatter.91.cloned.1.call-done = bf16[640,80]{0,1:T(8,128)(2,1)} async-done(((bf16[640,1280]{0,1:T(8,128)(2,1)}), bf16[640,80]{0,1:T(8,128)(2,1)}) %reduce-scatter.91.cloned.1.call-update) | async-done | bytes 102416 | tf_op jit(solution)/shard_map/reduce_scatter | solution.py:276
  2580.6 78.4 %reduce-scatter.89.cloned.1.call-done = bf16[640,80]{0,1:T(8,128)(2,1)} async-done(((bf16[640,1280]{0,1:T(8,128)(2,1)}), bf16[640,80]{0,1:T(8,128)(2,1)}) %reduce-scatter.89.cloned.1.call-update) | async-done | bytes 102416 | tf_op jit(solution)/shard_map/reduce_scatter | solution.py:276
  2737.4 78.3 %reduce-scatter.77.cloned.1.call-done = bf16[640,80]{0,1:T(8,128)(2,1)} async-done(((bf16[640,1280]{0,1:T(8,128)(2,1)}), bf16[640,80]{0,1:T(8,128)(2,1)}) %reduce-scatter.77.cloned.1.call-update) | async-done | bytes 102416 | tf_op jit(solution)/shard_map/reduce_scatter | solution.py:273
  2815.6 78.5 %reduce-scatter.75.cloned.1.call-done = bf16[640,80]{0,1:T(8,128)(2,1)} async-done(((bf16[640,1280]{0,1:T(8,128)(2,1)}), bf16[640,80]{0,1:T(8,128)(2,1)}) %reduce-scatter.75.cloned.1.call-update) | async-done | bytes 102416 | tf_op jit(solution)/shard_map/reduce_scatter | solution.py:273
  2894.1 78.4 %reduce-scatter.73.cloned.1.call-done = bf16[640,80]{0,1:T(8,128)(2,1)} async-done(((bf16[640,1280]{0,1:T(8,128)(2,1)}), bf16[640,80]{0,1:T(8,128)(2,1)}) %reduce-scatter.73.cloned.1.call-update) | async-done | bytes 102416 | tf_op jit(solution)/shard_map/reduce_scatter | solution.py:273
  2997.5 77.3 %all-reduce.10 = (bf16[1280]{0:T(1024)(128)(2,1)S(1)}, bf16[1280]{0:T(1024)(128)(2,1)S(1)}, bf16[1280]{0:T(1024)(128)(2,1)S(1)}, bf16[1280]{0:T(1024)(128)(2,1)S...) all-reduce(bf16[1280]{0:T(1024)(128)(2,1)S(1)} %get-tuple-element.7, ...), channel_id=37, replica_groups=mesh['ctx'=16,'tp'=2] {'ctx'}, use_global_device_ids=true, to_apply=%region_103.104.clone | all-reduce | flops 10240 | bytes 40960
  3156.7 78.2 %reduce-scatter.51.cloned.1.call-done = bf16[80,640]{1,0:T(8,128)(2,1)} async-done(((bf16[1280,640]{1,0:T(8,128)(2,1)}), bf16[80,640]{1,0:T(8,128)(2,1)}) %reduce-scatter.51.cloned.1.call-update) | async-done | bytes 102416 | tf_op jit(solution)/shard_map/reduce_scatter | solution.py:255
  3234.9 78.5 %reduce-scatter.49.cloned.1.call-done = bf16[80,640]{1,0:T(8,128)(2,1)} async-done(((bf16[1280,640]{1,0:T(8,128)(2,1)}), bf16[80,640]{1,0:T(8,128)(2,1)}) %reduce-scatter.49.cloned.1.call-update) | async-done | bytes 102416 | tf_op jit(solution)/shard_map/reduce_scatter | solution.py:255
  3391.6 78.3 %reduce-scatter.61.cloned.1.call-done = bf16[80,640]{1,0:T(8,128)(2,1)} async-done(((bf16[1280,640]{1,0:T(8,128)(2,1)}), bf16[80,640]{1,0:T(8,128)(2,1)}) %reduce-scatter.61.cloned.1.call-update) | async-done | bytes 102416 | tf_op jit(solution)/shard_map/reduce_scatter | solution.py:258
  3469.9 78.3 %reduce-scatter.59.cloned.1.call-done = bf16[80,640]{1,0:T(8,128)(2,1)} async-done(((bf16[1280,640]{1,0:T(8,128)(2,1)}), bf16[80,640]{1,0:T(8,128)(2,1)}) %reduce-scatter.59.cloned.1.call-update) | async-done | bytes 102416 | tf_op jit(solution)/shard_map/reduce_scatter | solution.py:258
  3548.2 78.4 %reduce-scatter.57.cloned.1.call-done = bf16[80,640]{1,0:T(8,128)(2,1)} async-done(((bf16[1280,640]{1,0:T(8,128)(2,1)}), bf16[80,640]{1,0:T(8,128)(2,1)}) %reduce-scatter.57.cloned.1.call-update) | async-done | bytes 102416 | tf_op jit(solution)/shard_map/reduce_scatter | solution.py:258
  3704.8 78.4 %reduce-scatter.69.cloned.1.call-done = bf16[80,640]{1,0:T(8,128)(2,1)} async-done(((bf16[1280,640]{1,0:T(8,128)(2,1)}), bf16[80,640]{1,0:T(8,128)(2,1)}) %reduce-scatter.69.cloned.1.call-update) | async-done | bytes 102416 | tf_op jit(solution)/shard_map/reduce_scatter | solution.py:261
  3783.2 78.2 %reduce-scatter.67.cloned.1.call-done = bf16[80,640]{1,0:T(8,128)(2,1)} async-done(((bf16[1280,640]{1,0:T(8,128)(2,1)}), bf16[80,640]{1,0:T(8,128)(2,1)}) %reduce-scatter.67.cloned.1.call-update) | async-done | bytes 102416 | tf_op jit(solution)/shard_map/reduce_scatter | solution.py:261
  3861.4 78.4 %reduce-scatter.65.cloned.1.call-done = bf16[80,640]{1,0:T(8,128)(2,1)} async-done(((bf16[1280,640]{1,0:T(8,128)(2,1)}), bf16[80,640]{1,0:T(8,128)(2,1)}) %reduce-scatter.65.cloned.1.call-update) | async-done | bytes 102416 | tf_op jit(solution)/shard_map/reduce_scatter | solution.py:261
  (1021 shorter events, 2312.8 us)
Async XLA Ops:
  1453.1 735.7 %reduce-scatter.87.cloned.1.call-start = ((), (), s32[]{:S(2)}) async-start(), calls=%async_computation.78 | async-start | bytes 1740800 | tf_op jit(solution)/shard_map/reduce_scatter | solution.py:264
  1455.2 812.0 %reduce-scatter.83.cloned.1.call-start = ((), (), s32[]{:S(2)}) async-start(), calls=%async_computation.76 | async-start | bytes 1740800 | tf_op jit(solution)/shard_map/reduce_scatter | solution.py:264
  1457.2 888.3 %reduce-scatter.81.cloned.1.call-start = ((), (), s32[]{:S(2)}) async-start(), calls=%async_computation.75 | async-start | bytes 1740800 | tf_op jit(solution)/shard_map/reduce_scatter | solution.py:264
  1459.3 964.5 %reduce-scatter.93.cloned.1.call-start = ((), (), s32[]{:S(2)}) async-start(), calls=%async_computation.81 | async-start | bytes 1740800 | tf_op jit(solution)/shard_map/reduce_scatter | solution.py:276
  1462.3 1040.1 %reduce-scatter.95.cloned.1.call-start = ((), (), s32[]{:S(2)}) async-start(), calls=%async_computation.82 | async-start | bytes 1740800 | tf_op jit(solution)/shard_map/reduce_scatter | solution.py:276
  1465.2 1115.4 %reduce-scatter.91.cloned.1.call-start = ((), (), s32[]{:S(2)}) async-start(), calls=%async_computation.80 | async-start | bytes 1740800 | tf_op jit(solution)/shard_map/reduce_scatter | solution.py:276
  1468.0 1191.0 %reduce-scatter.89.cloned.1.call-start = ((), (), s32[]{:S(2)}) async-start(), calls=%async_computation.79 | async-start | bytes 1740800 | tf_op jit(solution)/shard_map/reduce_scatter | solution.py:276
  1471.0 1266.4 %reduce-scatter.79.cloned.1.call-start = ((), (), s32[]{:S(2)}) async-start(), calls=%async_computation.74 | async-start | bytes 1740800 | tf_op jit(solution)/shard_map/reduce_scatter | solution.py:273
  1473.8 1341.9 %reduce-scatter.77.cloned.1.call-start = ((), (), s32[]{:S(2)}) async-start(), calls=%async_computation.73 | async-start | bytes 1740800 | tf_op jit(solution)/shard_map/reduce_scatter | solution.py:273
  1476.8 1417.3 %reduce-scatter.75.cloned.1.call-start = ((), (), s32[]{:S(2)}) async-start(), calls=%async_computation.72 | async-start | bytes 1740800 | tf_op jit(solution)/shard_map/reduce_scatter | solution.py:273
  1479.7 1492.9 %reduce-scatter.73.cloned.1.call-start = ((), (), s32[]{:S(2)}) async-start(), calls=%async_computation.71 | async-start | bytes 1740800 | tf_op jit(solution)/shard_map/reduce_scatter | solution.py:273
  1484.4 1511.0 %all-reduce.23.cloned.1.call-start = ((), (), s32[]{:S(2)}) async-start(), calls=%async_computation.83 | async-start | bytes 5242880 | tf_op jit(solution)/shard_map/psum | solution.py:127
  2036.7 1045.9 %reduce-scatter.55.cloned.1.call-start = ((), (), s32[]{:S(2)}) async-start(), calls=%async_computation.62 | async-start | bytes 1740800 | tf_op jit(solution)/shard_map/reduce_scatter | solution.py:255
  2041.9 1114.8 %reduce-scatter.53.cloned.1.call-start = ((), (), s32[]{:S(2)}) async-start(), calls=%async_computation.61 | async-start | bytes 1740800 | tf_op jit(solution)/shard_map/reduce_scatter | solution.py:255
  2046.0 1188.9 %reduce-scatter.51.cloned.1.call-start = ((), (), s32[]{:S(2)}) async-start(), calls=%async_computation.60 | async-start | bytes 1740800 | tf_op jit(solution)/shard_map/reduce_scatter | solution.py:255
  2050.1 1263.4 %reduce-scatter.49.cloned.1.call-start = ((), (), s32[]{:S(2)}) async-start(), calls=%async_computation.59 | async-start | bytes 1740800 | tf_op jit(solution)/shard_map/reduce_scatter | solution.py:255
  2054.3 1337.3 %reduce-scatter.63.cloned.1.call-start = ((), (), s32[]{:S(2)}) async-start(), calls=%async_computation.66 | async-start | bytes 1740800 | tf_op jit(solution)/shard_map/reduce_scatter | solution.py:258
  2054.9 1415.0 %reduce-scatter.61.cloned.1.call-start = ((), (), s32[]{:S(2)}) async-start(), calls=%async_computation.65 | async-start | bytes 1740800 | tf_op jit(solution)/shard_map/reduce_scatter | solution.py:258
  2055.5 1492.7 %reduce-scatter.59.cloned.1.call-start = ((), (), s32[]{:S(2)}) async-start(), calls=%async_computation.64 | async-start | bytes 1740800 | tf_op jit(solution)/shard_map/reduce_scatter | solution.py:258
  2056.1 1570.6 %reduce-scatter.57.cloned.1.call-start = ((), (), s32[]{:S(2)}) async-start(), calls=%async_computation.63 | async-start | bytes 1740800 | tf_op jit(solution)/shard_map/reduce_scatter | solution.py:258
  2056.8 1648.0 %reduce-scatter.71.cloned.1.call-start = ((), (), s32[]{:S(2)}) async-start(), calls=%async_computation.70 | async-start | bytes 1740800 | tf_op jit(solution)/shard_map/reduce_scatter | solution.py:261
  2057.4 1725.8 %reduce-scatter.69.cloned.1.call-start = ((), (), s32[]{:S(2)}) async-start(), calls=%async_computation.69 | async-start | bytes 1740800 | tf_op jit(solution)/shard_map/reduce_scatter | solution.py:261
  2058.1 1803.2 %reduce-scatter.67.cloned.1.call-start = ((), (), s32[]{:S(2)}) async-start(), calls=%async_computation.68 | async-start | bytes 1740800 | tf_op jit(solution)/shard_map/reduce_scatter | solution.py:261
  2058.7 1881.1 %reduce-scatter.65.cloned.1.call-start = ((), (), s32[]{:S(2)}) async-start(), calls=%async_computation.67 | async-start | bytes 1740800 | tf_op jit(solution)/shard_map/reduce_scatter | solution.py:261
  (236 other events, 17381.8 us)
Sparse Core Ops, SparseCore 0:
  199.0 84.0 all-gather.34
  488.1 84.0 all-gather.36
  575.1 83.7 all-gather.24
  662.0 83.7 all-gather.32
  1377.3 80.8 reduce-scatter.46
  1461.2 79.4 reduce-scatter.44
  1542.9 79.6 reduce-scatter.34
  1625.1 79.6 reduce-scatter.32
  1707.0 79.3 reduce-scatter.38
  1788.6 79.2 reduce-scatter.36
  1870.2 79.5 reduce-scatter.42
  1952.2 79.5 reduce-scatter.40
  2034.1 76.3 reduce-scatter.84
  2112.7 76.0 reduce-scatter.86
  2269.4 76.0 reduce-scatter.80
  2426.2 76.0 reduce-scatter.94
  2582.7 76.2 reduce-scatter.88
  2739.5 76.0 reduce-scatter.76
  2818.0 76.0 reduce-scatter.74
  2896.4 76.0 reduce-scatter.72
  2997.5 80.7 reduce-scatter.54
  3158.8 76.0 reduce-scatter.50
  3237.1 76.2 reduce-scatter.48
  3472.1 76.1 reduce-scatter.58
  (30 shorter events, 1839.7 us)
